TPU v7x, 32 devices: a whole 2x2x4 slice. The times are simulated.
32 devices in a mesh: radial: 1, mode: 32 (over z, y, x, core).
Axes of the slice: x: 2, y: 2, z: 4, core: 2. Of those that a mesh axis runs over, the one named last changes fastest.
Arguments:
- spectral_state: float32 [64, 3, 2, 2, 129], P('mode', None, 'radial'), may hold values from -6 to 6
- synthesis_table: bfloat16 [64, 129, 128], P('mode', None, 'radial'), may hold values from -0.03125 to 0.03125
- low_orders: int32 [64], replicated, may hold values from 0 to 63, each once
- diffusion: float32 [3], replicated, may hold values from 200 to 2000
- coupling: float32 [3], replicated, may hold values from 1 to 4
Outputs:
- updated: float32 [64, 3, 2, 2, 129], P('mode', None, 'radial')
Inputs may be any that keep to these rules, and one draw needn't show every extreme that they name: A permutation: pair j holds the orders low_orders[j] and 127 - low_orders[j].
All inputs are finite; a program needn't handle non-finite values.
Results may differ from a plain program's by a relative error of at most 0.0023.
The roundings to bfloat16 on the way count: a program that leaves them out, or rounds other values in their place, can miss the bound.
Values may be sent and summed in bfloat16 or wider, within the bound.
No kernel may reach another device: no remote copies, remote signals or barrier semaphores. Data moves between devices by JAX's collectives and lax.ppermute only.
A program may use at most 64 MiB of HBM per device.

v0:
```python
import math
import jax
import jax.numpy as jnp
from jax import lax
from jax.sharding import PartitionSpec as P

inner_radius = 0.538
shell_step = 1.0 / 2048.0
block_limit = 384


def with_halo(shard, sides, width):
    for axis, dim in sides:
        count, length = (lax.axis_size(axis), shard.shape[dim])
        up = [(i, (i + 1) % count) for i in range(count - 1)]
        down = [(j, i) for i, j in up]
        last = lax.slice_in_dim(shard, length - width, length, axis=dim)
        first = lax.slice_in_dim(shard, 0, width, axis=dim)
        before = lax.ppermute(last, axis, up)
        after = lax.ppermute(first, axis, down)
        shard = jnp.concatenate([before, shard, after], axis=dim)
    return shard


def pair_layout(lower_orders, rows_total):
    orders_total = rows_total - 1
    row_index = lax.iota(jnp.int32, rows_total)[None, :]
    lower_col = lower_orders[:, None]
    in_lower = row_index < orders_total - lower_col
    degree = jnp.where(in_lower, lower_col + row_index, row_index - 1)
    order_of = jnp.where(in_lower, lower_col, orders_total - 1 - lower_col)
    return (in_lower, degree, order_of)


def body(spectral_state, synthesis_table, low_orders, diffusion, coupling):
    synthesis_table = lax.all_gather(synthesis_table, "radial", axis=2, tiled=True)
    pairs_dev, field_count, shell_count, part_count, rows_total = spectral_state.shape
    half_lat = synthesis_table.shape[2]
    lat_total = 2 * half_lat
    orders_total = rows_total - 1
    lon_total = 3 * orders_total
    mode_count = lax.axis_size("mode")
    column_count = 4 * pairs_dev * mode_count
    own_lower = lax.dynamic_slice_in_dim(low_orders, lax.axis_index("mode") * pairs_dev, pairs_dev)
    in_lower, degree, order_of = pair_layout(own_lower, rows_total)
    parity_even = (degree + order_of) % 2 == 0
    order_mask = jnp.stack([in_lower, jnp.logical_not(in_lower)], axis=1)
    parity_mask = jnp.stack([parity_even, jnp.logical_not(parity_even)], axis=1)
    row_sign = jnp.where(parity_even, 1.0, -1.0).astype(jnp.float32)
    order_float = order_mask.astype(jnp.float32)
    coeffs = spectral_state.astype(jnp.bfloat16)
    all_lower = low_orders.reshape(mode_count, 1, pairs_dev, 1)
    partner = jnp.arange(2, dtype=jnp.int32).reshape(1, 1, 1, 2)
    column_order = jnp.where(partner == 0, all_lower, orders_total - 1 - all_lower)
    column_order = jnp.broadcast_to(column_order, (mode_count, 2, pairs_dev, 2)).reshape(
        column_count
    )
    cosine_rows = jnp.broadcast_to(
        jnp.arange(2, dtype=jnp.int32).reshape(1, 2, 1, 1) == 0, (mode_count, 2, pairs_dev, 2)
    ).reshape(column_count)
    synth_weight = jnp.where(column_order == 0, 1.0, 2.0).astype(jnp.float32)
    block_size = min(block_limit, lon_total)
    block_total = lon_total // block_size
    analysis_scale = 2.0 * math.sqrt(orders_total * rows_total / (lat_total * lon_total))
    spread = (
        coeffs[:, None, :, :, :, None, :]
        * parity_mask.astype(jnp.bfloat16)[:, :, None, None, None, None, :]
        * order_mask.astype(jnp.bfloat16)[:, None, None, None, None, :, :]
    )
    halves = jnp.einsum(
        "pqfsckr,prn->qnsfcpk", spread, synthesis_table, preferred_element_type=jnp.float32
    )
    northern = halves[0] + halves[1]
    southern = (halves[0] - halves[1])[::-1]
    joined = jnp.concatenate([northern, southern], axis=0).astype(jnp.bfloat16)
    pieces = lax.all_to_all(
        joined.reshape(lat_total, shell_count, coeffs.shape[1], 4 * pairs_dev),
        "mode",
        split_axis=0,
        concat_axis=3,
        tiled=True,
    )
    lat_dev = pieces.shape[0]
    item_count = pieces.shape[1]
    row_total = lat_dev * item_count * field_count
    weighted = pieces.reshape(row_total, column_count).astype(jnp.float32) * synth_weight[None, :]
    totals = jnp.zeros((row_total, column_count), jnp.float32)
    for block_at in range(block_total):
        longitude = block_at * block_size + lax.iota(jnp.int32, block_size)
        phase_index = column_order[:, None] * longitude[None, :] % lon_total
        angles = phase_index.astype(jnp.float32) * (2.0 * math.pi / lon_total)
        wave_table = jnp.where(cosine_rows[:, None], jnp.cos(angles), -jnp.sin(angles))
        values = jnp.dot(weighted, wave_table, precision=lax.Precision.HIGHEST)
        values = values.reshape(lat_dev, item_count, field_count, block_size)
        products = jnp.stack(
            [
                values[:, :, 0] * values[:, :, 1],
                values[:, :, 0] * values[:, :, 2],
                values[:, :, 1] * values[:, :, 2],
            ],
            axis=2,
        )
        totals = totals + lax.dot_general(
            products.reshape(row_total, block_size),
            wave_table,
            (((1,), (1,)), ((), ())),
            precision=lax.Precision.HIGHEST,
        )
    answers = (totals * analysis_scale).astype(jnp.bfloat16)
    returned = lax.all_to_all(
        answers.reshape(lat_dev, item_count, field_count, column_count),
        "mode",
        split_axis=3,
        concat_axis=0,
        tiled=True,
    )
    subset_fields = returned.shape[2]
    arranged = returned.reshape(lat_total, shell_count, subset_fields, part_count, pairs_dev, 2)
    from_north = jnp.einsum(
        "prn,nsfcpk->pkfscr",
        synthesis_table,
        arranged[:half_lat],
        preferred_element_type=jnp.float32,
    )
    from_south = jnp.einsum(
        "prn,nsfcpk->pkfscr",
        synthesis_table,
        arranged[half_lat:][::-1],
        preferred_element_type=jnp.float32,
    )
    combined = from_north + row_sign[:, None, None, None, None, :] * from_south
    nonlinear = jnp.sum(combined * order_float[:, :, None, None, None, :], axis=1)
    radial_at = lax.axis_index("radial")
    rate_col = diffusion.reshape(1, field_count, 1, 1)
    strength = coupling.reshape(1, field_count, 1, 1)
    degree_term = degree.astype(jnp.float32)
    degree_term = (degree_term * (degree_term + 1.0))[:, None, None, :] * (shell_step * shell_step)
    with_edges = with_halo(spectral_state.astype(jnp.bfloat16), (("radial", 2),), 1).astype(
        spectral_state.dtype
    )
    diagonals = []
    drives = []
    for shell_at in range(shell_count):
        radius = (
            inner_radius
            + ((radial_at * shell_count + shell_at).astype(jnp.float32) + 0.5) * shell_step
        )
        damping = degree_term / (radius * radius)
        middle = with_edges[:, :, shell_at + 1]
        laplace = (
            with_edges[:, :, shell_at + 2]
            - 2.0 * middle
            + with_edges[:, :, shell_at]
            - damping * middle
        )
        drives.append(middle + rate_col * (laplace + strength * nonlinear[:, :, shell_at]))
        diagonals.append(1.0 + rate_col * (2.0 + damping))
    narrow_zero = jnp.zeros(diagonals[0].shape, jnp.float32)
    wide_zero = jnp.zeros(drives[0].shape, jnp.float32)
    pivot_prev = narrow_zero
    carry_u, carry_v, carry_w = (wide_zero, narrow_zero, narrow_zero)
    pivots, sweep_u, sweep_v, sweep_w = ([], [], [], [])
    for shell_at in range(shell_count):
        denom_at = diagonals[shell_at] + rate_col * pivot_prev
        pivot_prev = -rate_col / denom_at
        first_drive = rate_col if shell_at == 0 else 0.0
        last_drive = rate_col if shell_at == shell_count - 1 else 0.0
        carry_u = (drives[shell_at] + rate_col * carry_u) / denom_at
        carry_v = (first_drive + rate_col * carry_v) / denom_at
        carry_w = (last_drive + rate_col * carry_w) / denom_at
        pivots.append(pivot_prev)
        sweep_u.append(carry_u)
        sweep_v.append(carry_v)
        sweep_w.append(carry_w)
    solved_u, solved_v, solved_w = ([sweep_u[-1]], [sweep_v[-1]], [sweep_w[-1]])
    shell_at = 0
    solved_u.insert(0, sweep_u[shell_at] - pivots[shell_at] * solved_u[0])
    solved_v.insert(0, sweep_v[shell_at] - pivots[shell_at] * solved_v[0])
    solved_w.insert(0, sweep_w[shell_at] - pivots[shell_at] * solved_w[0])
    first_u, last_u = (solved_u[0], solved_u[-1])
    first_v, last_v = (solved_v[0], solved_v[-1])
    first_w, last_w = (solved_w[0], solved_w[-1])
    wide_rows = jnp.stack([first_u, last_u])[None]
    narrow_rows = jnp.stack([first_v, first_w, last_v, last_w])[None]
    wide_all, narrow_all = (
        lax.all_gather(wide_rows, "radial", axis=0, tiled=True),
        lax.all_gather(narrow_rows, "radial", axis=0, tiled=True),
    )
    chain_count = lax.axis_size("radial")
    alpha_now, beta_now = (wide_zero, narrow_zero)
    alphas, betas = ([], [])
    for member in range(chain_count):
        alphas.append(alpha_now)
        betas.append(beta_now)
        peer_first_u, peer_last_u = (wide_all[member, 0], wide_all[member, 1])
        peer_first_v, peer_first_w = (narrow_all[member, 0], narrow_all[member, 1])
        peer_last_v, peer_last_w = (narrow_all[member, 2], narrow_all[member, 3])
        shrink = 1.0 - peer_first_v * beta_now
        alpha_new = (
            peer_last_u
            - peer_last_u * peer_first_v * beta_now
            + peer_last_v * alpha_now
            + peer_last_v * peer_first_u * beta_now
        ) / shrink
        beta_new = (
            peer_last_w
            - peer_last_w * peer_first_v * beta_now
            + peer_last_v * peer_first_w * beta_now
        ) / shrink
        alpha_now, beta_now = (alpha_new, beta_new)
    next_first = wide_zero
    firsts = [None] * chain_count
    nexts = [None] * chain_count
    for member in range(chain_count - 1, -1, -1):
        nexts[member] = next_first
        peer_first_u = wide_all[member, 0]
        peer_first_v, peer_first_w = (narrow_all[member, 0], narrow_all[member, 1])
        next_first = (peer_first_u + peer_first_v * alphas[member] + peer_first_w * next_first) / (
            1.0 - peer_first_v * betas[member]
        )
        firsts[member] = next_first
    alpha_prev = lax.dynamic_index_in_dim(jnp.stack(alphas), radial_at, 0, keepdims=False)
    beta_prev = lax.dynamic_index_in_dim(jnp.stack(betas), radial_at, 0, keepdims=False)
    own_first = lax.dynamic_index_in_dim(jnp.stack(firsts), radial_at, 0, keepdims=False)
    next_first = lax.dynamic_index_in_dim(jnp.stack(nexts), radial_at, 0, keepdims=False)
    prev_last = alpha_prev + beta_prev * own_first
    outputs = []
    for shell_at in range(shell_count):
        outputs.append(
            solved_u[shell_at] + prev_last * solved_v[shell_at] + next_first * solved_w[shell_at]
        )
    return jnp.stack(outputs, axis=2)


def solution(mesh):
    placed = (P("mode", None, "radial", None, None), P("mode", None, "radial"), P(), P(), P())
    return jax.shard_map(
        body,
        mesh=mesh,
        in_specs=placed,
        out_specs=P("mode", None, "radial", None, None),
        check_vma=False,
    )
```

profile of v0, /device:TPU:0, one launch (start us, length us, event | category | flops | bytes accessed | tf_op | source)
XLA Modules:
  0.0 39.1 jit_solution(3791041279454272241)
XLA Ops:
  0.0 0.7 %copy-done.4 = s32[64]{0:T(128)S(1)} copy-done((s32[64]{0:T(128)S(1)}, s32[64]{0:T(128)}, u32[]{:S(2)}) %copy-start.4) | copy-done | bytes 280
  1.0 0.2 convolution_bitcast_fusion
  1.4 0.4 copy.85
  1.8 1.0 %reshape.1034 = bf16[32,2,192]{2,1,0:T(2,128)(2,1)} reshape(bf16[256,3,2,8]{3,2,1,0:T(2,128)(2,1)S(1)} %bitcast.154) | data formatting | bytes 49152
  2.8 7.3 %all-to-all-start = ((bf16[32,2,192]{2,1,0:T(2,128)(2,1)}), bf16[32,2,192]{2,1,0:T(2,128)(2,1)S(1)}, u32[]{:S(2)}, u32[]{:S(2)}) async-start(bf16[32,2,192]{2,1,0:T(2,128)(2,1)} %reshape.1034), calls=%async_computation | async-start | bytes 65536 | tf_op jit(solution)/shard_map/all_to_all | solution.py:76
  10.1 0.7 %collective-permute-start = (bf16[2,3,1,2,129]{4,1,3,0,2:T(4,128)(2,1)S(1)}, bf16[2,3,1,2,129]{4,1,3,0,2:T(4,128)(2,1)S(1)}, u32[]{:S(2)}, u32[]{:S(2)}) collective-permute-start(bf16[2,3,1,2,129]{4,1,3,0,2:T(4,128)(2,1)S(1)} %get-tuple-element.20), channel_id=1, source_target_pairs={} | collective-permute-start | bytes 9296 | tf_op jit(solution)/shard_map/ppermute | solution.py:19
  10.8 0.7 %collective-permute-start.1 = (bf16[2,3,1,2,129]{4,1,3,0,2:T(4,128)(2,1)S(1)}, bf16[2,3,1,2,129]{4,1,3,0,2:T(4,128)(2,1)S(1)}, u32[]{:S(2)}, u32[]{:S(2)}) collective-permute-start(bf16[2,3,1,2,129]{4,1,3,0,2:T(4,128)(2,1)S(1)} %get-tuple-element.21), channel_id=1, source_target_pairs={} | collective-permute-start | bytes 9296 | tf_op jit(solution)/shard_map/ppermute | solution.py:20
  11.7 0.6 %copy-done.2 = f32[3]{0:T(128)S(1)} copy-done((f32[3]{0:T(128)S(1)}, f32[3]{0:T(128)}, u32[]{:S(2)}) %copy-start.2) | copy-done | bytes 36
  12.6 0.1 reshape.1025
  12.9 0.1 broadcast_in_dim.121
  13.0 4.3 %all-to-all-done = bf16[32,2,192]{2,1,0:T(2,128)(2,1)S(1)} async-done(((bf16[32,2,192]{2,1,0:T(2,128)(2,1)}), bf16[32,2,192]{2,1,0:T(2,128)(2,1)S(1)}, u32[]{:S(2)}, u32[]{:S(2)}) %all-to-all-start) | async-done | bytes 24608 | tf_op jit(solution)/shard_map/all_to_all | solution.py:76
  17.3 0.3 reshape.1035
  17.7 0.3 copy.86
  17.9 0.5 %reshape.1029 = f32[32,8,2,3,8]{1,0,4,3,2:T(8,128)S(1)} reshape(bf16[256,2,3,8]{0,3,2,1:T(8,128)(2,1)S(1)} %copy.86) | data formatting | bytes 73728 | tf_op jit(solution)/shard_map/convert_element_type | solution.py:86
  18.4 0.9 %copy.87 = f32[8,2,3,32,8]{4,3,0,2,1:T(8,128)S(1)} copy(f32[8,2,3,32,8]{0,3,4,2,1:T(8,128)S(1)} %bitcast.152) | data formatting | bytes 98304 | tf_op jit(solution)/shard_map/convert_element_type | solution.py:86
  19.3 0.4 %reshape.1028 = f32[8,2,3,256]{3,0,2,1:T(8,128)S(1)} reshape(f32[8,2,3,32,8]{4,3,0,2,1:T(8,128)S(1)} %copy.87) | data formatting | bytes 98304 | tf_op jit(solution)/shard_map/convert_element_type | solution.py:86
  19.7 2.0 %fusion.6 = f32[8,2,3,384]{3,0,2,1:T(8,128)S(1)} fusion(s32[256]{0:T(256)S(1)} %reshape.1025, pred[256]{0:T(512)(128)(4,1)S(1)} %broadcast_in_dim.121, f32[8,2,3,256]{3,0,2,1:T(8,128)S(1)} %reshape.1028, f32[256]{0:T(256)S(1)} %compare_select_fusion.5), kind=kOutput, calls=%fused_computation.10 | convolution fusion | flops 57716736 | bytes 125184 | tf_op jit(solution)/shard_map/dot_general | solution.py:93
  21.8 2.1 %fusion.3 = bf16[48,256]{1,0:T(8,128)(2,1)S(1)} fusion(f32[48,384]{1,0:T(8,128)S(1)} %reshape.1026, s32[256]{0:T(256)S(1)} %reshape.1025, pred[256]{0:T(512)(128)(4,1)S(1)} %broadcast_in_dim.121), kind=kOutput, calls=%fused_computation.6 | convolution fusion | flops 57729024 | bytes 99584 | tf_op jit(solution)/shard_map/dot_general | solution.py:103
  24.0 0.4 copy.89
  24.4 1.0 %reshape.1036 = bf16[32,2,192]{2,1,0:T(2,128)(2,1)} reshape(bf16[256,3,2,8]{3,2,1,0:T(2,128)(2,1)S(1)} %bitcast.157) | data formatting | bytes 49152
  25.4 2.5 %all-to-all-start.1 = ((bf16[32,2,192]{2,1,0:T(2,128)(2,1)}), bf16[32,2,192]{2,1,0:T(2,128)(2,1)S(1)}, u32[]{:S(2)}, u32[]{:S(2)}) async-start(bf16[32,2,192]{2,1,0:T(2,128)(2,1)} %reshape.1036), calls=%async_computation.1 | async-start | bytes 65536 | tf_op jit(solution)/shard_map/all_to_all | solution.py:110
  28.0 7.2 %all-to-all-done.1 = bf16[32,2,192]{2,1,0:T(2,128)(2,1)S(1)} async-done(((bf16[32,2,192]{2,1,0:T(2,128)(2,1)}), bf16[32,2,192]{2,1,0:T(2,128)(2,1)S(1)}, u32[]{:S(2)}, u32[]{:S(2)}) %all-to-all-start.1) | async-done | bytes 24608 | tf_op jit(solution)/shard_map/all_to_all | solution.py:110
  35.2 0.3 reshape.1037
  35.5 0.6 %copy.108 = bf16[8,2,3,32,8]{4,3,0,2,1:T(8,128)(2,1)S(1)} copy(bf16[8,2,3,32,8]{0,1,2,4,3:T(2,128)(2,1)S(1)} %bitcast.156) | data formatting | bytes 49152 | tf_op jit(solution)/shard_map/all_to_all | solution.py:110
  36.1 0.3 copy.91
  36.4 0.2 slice.78
  36.6 0.3 copy.94
  36.9 0.2 slice.80
  37.2 0.2 fusion.23
  37.4 0.2 fusion.2
  37.6 0.6 %copy-done.3 = f32[3]{0:T(128)S(1)} copy-done((f32[3]{0:T(128)S(1)}, f32[3]{0:T(128)}, u32[]{:S(2)}) %copy-start.3) | copy-done | bytes 36
  38.5 0.6 %copy.99 = f32[2,3,2,2,129]{4,3,2,1,0:T(2,128)} copy(f32[2,3,2,2,129]{4,1,3,0,2:T(4,128)S(1)} %pad_maximum_fusion.1) | data formatting | bytes 24768 | tf_op jit(solution)/shard_map/stack | solution.py:232
  (48 shorter events, 1.6 us)
Async XLA Ops:
  0.0 1.0 %copy-start = (bf16[2,129,128]{2,0,1:T(2,128)(2,1)S(1)}, bf16[2,129,128]{2,0,1:T(2,128)(2,1)}, u32[]{:S(2)}) copy-start(bf16[2,129,128]{2,0,1:T(2,128)(2,1)} %param.6) | copy-start | bytes 198148
  0.0 0.7 %copy-start.4 = (s32[64]{0:T(128)S(1)}, s32[64]{0:T(128)}, u32[]{:S(2)}) copy-start(s32[64]{0:T(128)} %param.7) | copy-start | bytes 772
  0.0 0.9 %copy-start.1 = (f32[2,3,2,2,129]{4,3,2,1,0:T(2,128)S(1)}, f32[2,3,2,2,129]{4,3,2,1,0:T(2,128)}, u32[]{:S(2)}) copy-start(f32[2,3,2,2,129]{4,3,2,1,0:T(2,128)} %param.5) | copy-start | bytes 37156
  2.8 14.6 %all-to-all-start = ((bf16[32,2,192]{2,1,0:T(2,128)(2,1)}), bf16[32,2,192]{2,1,0:T(2,128)(2,1)S(1)}, u32[]{:S(2)}, u32[]{:S(2)}) async-start(bf16[32,2,192]{2,1,0:T(2,128)(2,1)} %reshape.1034), calls=%async_computation | async-start | bytes 65536 | tf_op jit(solution)/shard_map/all_to_all | solution.py:76
  10.1 17.8 %collective-permute-start = (bf16[2,3,1,2,129]{4,1,3,0,2:T(4,128)(2,1)S(1)}, bf16[2,3,1,2,129]{4,1,3,0,2:T(4,128)(2,1)S(1)}, u32[]{:S(2)}, u32[]{:S(2)}) collective-permute-start(bf16[2,3,1,2,129]{4,1,3,0,2:T(4,128)(2,1)S(1)} %get-tuple-element.20), channel_id=1, source_target_pairs={} | collective-permute-start | bytes 9296 | tf_op jit(solution)/shard_map/ppermute | solution.py:19
  10.8 17.2 %collective-permute-start.1 = (bf16[2,3,1,2,129]{4,1,3,0,2:T(4,128)(2,1)S(1)}, bf16[2,3,1,2,129]{4,1,3,0,2:T(4,128)(2,1)S(1)}, u32[]{:S(2)}, u32[]{:S(2)}) collective-permute-start(bf16[2,3,1,2,129]{4,1,3,0,2:T(4,128)(2,1)S(1)} %get-tuple-element.21), channel_id=1, source_target_pairs={} | collective-permute-start | bytes 9296 | tf_op jit(solution)/shard_map/ppermute | solution.py:20
  11.6 0.7 %copy-start.2 = (f32[3]{0:T(128)S(1)}, f32[3]{0:T(128)}, u32[]{:S(2)}) copy-start(f32[3]{0:T(128)} %param.8) | copy-start | bytes 40
  25.4 9.8 %all-to-all-start.1 = ((bf16[32,2,192]{2,1,0:T(2,128)(2,1)}), bf16[32,2,192]{2,1,0:T(2,128)(2,1)S(1)}, u32[]{:S(2)}, u32[]{:S(2)}) async-start(bf16[32,2,192]{2,1,0:T(2,128)(2,1)} %reshape.1036), calls=%async_computation.1 | async-start | bytes 65536 | tf_op jit(solution)/shard_map/all_to_all | solution.py:110
  37.6 0.7 %copy-start.3 = (f32[3]{0:T(128)S(1)}, f32[3]{0:T(128)}, u32[]{:S(2)}) copy-start(f32[3]{0:T(128)} %param.9) | copy-start | bytes 40
where the time goes:
time: 39.4 us; the launch traced here: 39.1 us
  waiting for transfers between devices  11.5 us (29%)
  starting transfers between devices  11.2 us (28%)
  local copies, waits for them, and re-layouts  10.3 us (26%)
  matrix products  4.71 us (12%)
  other arithmetic  1.02 us (3%)
  between operations  0.42 us (1%)
    all_to_all x1, starting transfers between devices, body(): lax.all_to_all(joined.reshape(lat_total, shell_count, coeffs.shape[1], 4...  7.33 us
    all_to_all x1, waiting for transfers between devices, body(): lax.all_to_all(answers.reshape(lat_dev, item_count, field_count, column_c...  7.2 us
    unnamed x15, local copies, waits for them, and re-layouts  4.52 us
    all_to_all x1, waiting for transfers between devices, body(): lax.all_to_all(joined.reshape(lat_total, shell_count, coeffs.shape[1], 4...  4.32 us
    all_to_all x1, starting transfers between devices, body(): lax.all_to_all(answers.reshape(lat_dev, item_count, field_count, column_c...  2.52 us
    dot_general x1, matrix products, body(): lax.dot_general(products.reshape(row_total, block_size), wave_table, (((1...  2.15 us
    dot_general x1, matrix products, body(): values = jnp.dot(weighted, wave_table, precision=lax.Precision.HIGHEST)  2.03 us
    convert_element_type x3, local copies, waits for them, and re-layouts, body(): pieces.reshape(row_total, column_count).astype(jnp.float32)  1.73 us
  transfers between devices with their start and end apart: 4, of which 2 were waited for; matrix products, arithmetic and copies ran while one was open for 23% of the time, Pallas kernels for 0%

commit v1 on v0

--- a/solution.py
+++ b/solution.py
@@ -107,12 +107,20 @@
             precision=lax.Precision.HIGHEST,
         )
     answers = (totals * analysis_scale).astype(jnp.bfloat16)
-    returned = lax.all_to_all(
-        answers.reshape(lat_dev, item_count, field_count, column_count),
-        "mode",
-        split_axis=3,
-        concat_axis=0,
-        tiled=True,
+    returned = jnp.concatenate(
+        lax.all_to_all(
+            jnp.stack(
+                jnp.split(
+                    answers.reshape(lat_dev, item_count, field_count, column_count),
+                    lax.axis_size("mode"),
+                    axis=3,
+                )
+            ),
+            "mode",
+            0,
+            0,
+        ),
+        axis=0,
     )
     subset_fields = returned.shape[2]
     arranged = returned.reshape(lat_total, shell_count, subset_fields, part_count, pairs_dev, 2)

time: 39.4 us -> 41.2 us (1.046)
  local copies, waits for them, and re-layouts: 10.3 us -> 12 us
    unnamed x15 -> x46, local copies, waits for them, and re-layouts: 4.52 us -> 7.14 us
    all_to_all x1 -> x0, local copies, waits for them, and re-layouts: 0.55 us -> none  [body(): lax.all_to_all(answers.reshape(lat_dev, item_count, field_count, column_c...]
  transfers between devices with their start and end apart: 4 -> 4, of which waited for: 2 -> 2; matrix products, arithmetic and copies ran while one was open for 23% -> 28% of each run, Pallas kernels for 0% -> 0%
where the time goes in v1:
time: 41.2 us; the launch traced here: 41 us
  local copies, waits for them, and re-layouts  12 us (29%)
  waiting for transfers between devices  11.5 us (28%)
  starting transfers between devices  11.2 us (27%)
  matrix products  4.71 us (11%)
  other arithmetic  1.02 us (2%)
  between operations  0.54 us (1%)
    all_to_all x1, starting transfers between devices, body(): lax.all_to_all(joined.reshape(lat_total, shell_count, coeffs.shape[1], 4...  7.33 us
    all_to_all x1, waiting for transfers between devices, body(): lax.all_to_all(jnp.stack(jnp.split(answers.reshape(lat_dev, item_count, f...  7.2 us
    unnamed x46, local copies, waits for them, and re-layouts  7.14 us
    all_to_all x1, waiting for transfers between devices, body(): lax.all_to_all(joined.reshape(lat_total, shell_count, coeffs.shape[1], 4...  4.32 us
    all_to_all x1, starting transfers between devices, body(): lax.all_to_all(jnp.stack(jnp.split(answers.reshape(lat_dev, item_count, f...  2.52 us
    dot_general x1, matrix products, body(): lax.dot_general(products.reshape(row_total, block_size), wave_table, (((1...  2.15 us
    dot_general x1, matrix products, body(): values = jnp.dot(weighted, wave_table, precision=lax.Precision.HIGHEST)  2.03 us
    convert_element_type x3, local copies, waits for them, and re-layouts, body(): pieces.reshape(row_total, column_count).astype(jnp.float32)  1.73 us
  transfers between devices with their start and end apart: 4, of which 2 were waited for; matrix products, arithmetic and copies ran while one was open for 28% of the time, Pallas kernels for 0%

profile of v1, /device:TPU:0, one launch (start us, length us, event | category | flops | bytes accessed | tf_op | source)
XLA Modules:
  0.0 41.0 jit_solution(5366070116452455514)
XLA Ops:
  0.0 0.7 %copy-done.4 = s32[64]{0:T(128)S(1)} copy-done((s32[64]{0:T(128)S(1)}, s32[64]{0:T(128)}, u32[]{:S(2)}) %copy-start.4) | copy-done | bytes 280
  1.0 0.2 convolution_bitcast_fusion
  1.4 0.4 copy.165
  1.8 1.0 %reshape.1032 = bf16[32,2,192]{2,1,0:T(2,128)(2,1)} reshape(bf16[256,3,2,8]{3,2,1,0:T(2,128)(2,1)S(1)} %bitcast.282) | data formatting | bytes 49152
  2.8 7.3 %all-to-all-start = ((bf16[32,2,192]{2,1,0:T(2,128)(2,1)}), bf16[32,2,192]{2,1,0:T(2,128)(2,1)S(1)}, u32[]{:S(2)}, u32[]{:S(2)}) async-start(bf16[32,2,192]{2,1,0:T(2,128)(2,1)} %reshape.1032), calls=%async_computation | async-start | bytes 65536 | tf_op jit(solution)/shard_map/all_to_all | solution.py:76
  10.1 0.7 %collective-permute-start = (bf16[2,3,1,2,129]{4,1,3,0,2:T(4,128)(2,1)S(1)}, bf16[2,3,1,2,129]{4,1,3,0,2:T(4,128)(2,1)S(1)}, u32[]{:S(2)}, u32[]{:S(2)}) collective-permute-start(bf16[2,3,1,2,129]{4,1,3,0,2:T(4,128)(2,1)S(1)} %get-tuple-element.20), channel_id=1, source_target_pairs={} | collective-permute-start | bytes 9296 | tf_op jit(solution)/shard_map/ppermute | solution.py:19
  10.8 0.7 %collective-permute-start.1 = (bf16[2,3,1,2,129]{4,1,3,0,2:T(4,128)(2,1)S(1)}, bf16[2,3,1,2,129]{4,1,3,0,2:T(4,128)(2,1)S(1)}, u32[]{:S(2)}, u32[]{:S(2)}) collective-permute-start(bf16[2,3,1,2,129]{4,1,3,0,2:T(4,128)(2,1)S(1)} %get-tuple-element.21), channel_id=1, source_target_pairs={} | collective-permute-start | bytes 9296 | tf_op jit(solution)/shard_map/ppermute | solution.py:20
  11.7 0.6 %copy-done.2 = f32[3]{0:T(128)S(1)} copy-done((f32[3]{0:T(128)S(1)}, f32[3]{0:T(128)}, u32[]{:S(2)}) %copy-start.2) | copy-done | bytes 36
  12.5 0.1 broadcast_select_fusion
  12.6 0.1 reshape.1023
  12.9 0.1 broadcast_in_dim.121
  13.0 4.3 %all-to-all-done = bf16[32,2,192]{2,1,0:T(2,128)(2,1)S(1)} async-done(((bf16[32,2,192]{2,1,0:T(2,128)(2,1)}), bf16[32,2,192]{2,1,0:T(2,128)(2,1)S(1)}, u32[]{:S(2)}, u32[]{:S(2)}) %all-to-all-start) | async-done | bytes 24608 | tf_op jit(solution)/shard_map/all_to_all | solution.py:76
  17.3 0.3 reshape.1033
  17.7 0.3 copy.166
  17.9 0.5 %reshape.1027 = f32[32,8,2,3,8]{1,0,4,3,2:T(8,128)S(1)} reshape(bf16[256,2,3,8]{0,3,2,1:T(8,128)(2,1)S(1)} %copy.166) | data formatting | bytes 73728 | tf_op jit(solution)/shard_map/convert_element_type | solution.py:86
  18.4 0.9 %copy.167 = f32[8,2,3,32,8]{4,3,0,2,1:T(8,128)S(1)} copy(f32[8,2,3,32,8]{0,3,4,2,1:T(8,128)S(1)} %bitcast.280) | data formatting | bytes 98304 | tf_op jit(solution)/shard_map/convert_element_type | solution.py:86
  19.3 0.4 reshape.1026
  19.7 2.0 %fusion.6 = f32[8,2,3,384]{3,0,2,1:T(8,128)S(1)} fusion(s32[256]{0:T(256)S(1)} %reshape.1023, pred[256]{0:T(512)(128)(4,1)S(1)} %broadcast_in_dim.121, f32[8,2,3,256]{3,0,2,1:T(8,128)S(1)} %reshape.1026, f32[256]{0:T(256)S(1)} %compare_select_fusion.5), kind=kOutput, calls=%fused_computation.10 | convolution fusion | flops 57716736 | bytes 125184 | tf_op jit(solution)/shard_map/dot_general | solution.py:93
  21.8 2.1 %fusion.3 = bf16[48,256]{1,0:T(8,128)(2,1)S(1)} fusion(f32[48,384]{1,0:T(8,128)S(1)} %reshape.1024, s32[256]{0:T(256)S(1)} %reshape.1023, pred[256]{0:T(512)(128)(4,1)S(1)} %broadcast_in_dim.121), kind=kOutput, calls=%fused_computation.6 | convolution fusion | flops 57729024 | bytes 99584 | tf_op jit(solution)/shard_map/dot_general | solution.py:103
  26.9 1.0 %reshape.1034 = bf16[32,2,192]{2,1,0:T(2,128)(2,1)} reshape(bf16[32,2,3,8,8]{4,3,2,1,0:T(8,128)(2,1)S(1)} %bitcast.284) | data formatting | bytes 49152
  27.9 2.5 %all-to-all-start.1 = ((bf16[32,2,192]{2,1,0:T(2,128)(2,1)}), bf16[32,2,192]{2,1,0:T(2,128)(2,1)S(1)}, u32[]{:S(2)}, u32[]{:S(2)}) async-start(bf16[32,2,192]{2,1,0:T(2,128)(2,1)} %reshape.1034), calls=%async_computation.1 | async-start | bytes 65536 | tf_op jit(solution)/shard_map/all_to_all | solution.py:111
  30.5 7.2 %all-to-all-done.1 = bf16[32,2,192]{2,1,0:T(2,128)(2,1)S(1)} async-done(((bf16[32,2,192]{2,1,0:T(2,128)(2,1)}), bf16[32,2,192]{2,1,0:T(2,128)(2,1)S(1)}, u32[]{:S(2)}, u32[]{:S(2)}) %all-to-all-start.1) | async-done | bytes 24608 | tf_op jit(solution)/shard_map/all_to_all | solution.py:111
  37.7 0.3 reshape.1035
  38.1 0.2 copy.170
  38.3 0.2 slice.78
  38.5 0.2 copy.173
  38.7 0.2 slice.80
  38.9 0.1 rev.7
  39.1 0.2 fusion.23
  39.2 0.2 fusion.2
  39.4 0.6 %copy-done.3 = f32[3]{0:T(128)S(1)} copy-done((f32[3]{0:T(128)S(1)}, f32[3]{0:T(128)}, u32[]{:S(2)}) %copy-start.3) | copy-done | bytes 36
  40.3 0.6 %copy.178 = f32[2,3,2,2,129]{4,3,2,1,0:T(2,128)} copy(f32[2,3,2,2,129]{4,1,3,0,2:T(4,128)S(1)} %pad_maximum_fusion.1) | data formatting | bytes 24768 | tf_op jit(solution)/shard_map/stack | solution.py:240
  (79 shorter events, 4.1 us)
Async XLA Ops:
  0.0 1.0 %copy-start = (bf16[2,129,128]{2,0,1:T(2,128)(2,1)S(1)}, bf16[2,129,128]{2,0,1:T(2,128)(2,1)}, u32[]{:S(2)}) copy-start(bf16[2,129,128]{2,0,1:T(2,128)(2,1)} %param.6) | copy-start | bytes 198148
  0.0 0.7 %copy-start.4 = (s32[64]{0:T(128)S(1)}, s32[64]{0:T(128)}, u32[]{:S(2)}) copy-start(s32[64]{0:T(128)} %param.7) | copy-start | bytes 772
  0.0 0.9 %copy-start.1 = (f32[2,3,2,2,129]{4,3,2,1,0:T(2,128)S(1)}, f32[2,3,2,2,129]{4,3,2,1,0:T(2,128)}, u32[]{:S(2)}) copy-start(f32[2,3,2,2,129]{4,3,2,1,0:T(2,128)} %param.5) | copy-start | bytes 37156
  2.8 14.6 %all-to-all-start = ((bf16[32,2,192]{2,1,0:T(2,128)(2,1)}), bf16[32,2,192]{2,1,0:T(2,128)(2,1)S(1)}, u32[]{:S(2)}, u32[]{:S(2)}) async-start(bf16[32,2,192]{2,1,0:T(2,128)(2,1)} %reshape.1032), calls=%async_computation | async-start | bytes 65536 | tf_op jit(solution)/shard_map/all_to_all | solution.py:76
  10.1 20.3 %collective-permute-start = (bf16[2,3,1,2,129]{4,1,3,0,2:T(4,128)(2,1)S(1)}, bf16[2,3,1,2,129]{4,1,3,0,2:T(4,128)(2,1)S(1)}, u32[]{:S(2)}, u32[]{:S(2)}) collective-permute-start(bf16[2,3,1,2,129]{4,1,3,0,2:T(4,128)(2,1)S(1)} %get-tuple-element.20), channel_id=1, source_target_pairs={} | collective-permute-start | bytes 9296 | tf_op jit(solution)/shard_map/ppermute | solution.py:19
  10.8 19.7 %collective-permute-start.1 = (bf16[2,3,1,2,129]{4,1,3,0,2:T(4,128)(2,1)S(1)}, bf16[2,3,1,2,129]{4,1,3,0,2:T(4,128)(2,1)S(1)}, u32[]{:S(2)}, u32[]{:S(2)}) collective-permute-start(bf16[2,3,1,2,129]{4,1,3,0,2:T(4,128)(2,1)S(1)} %get-tuple-element.21), channel_id=1, source_target_pairs={} | collective-permute-start | bytes 9296 | tf_op jit(solution)/shard_map/ppermute | solution.py:20
  11.6 0.7 %copy-start.2 = (f32[3]{0:T(128)S(1)}, f32[3]{0:T(128)}, u32[]{:S(2)}) copy-start(f32[3]{0:T(128)} %param.8) | copy-start | bytes 40
  27.9 9.8 %all-to-all-start.1 = ((bf16[32,2,192]{2,1,0:T(2,128)(2,1)}), bf16[32,2,192]{2,1,0:T(2,128)(2,1)S(1)}, u32[]{:S(2)}, u32[]{:S(2)}) async-start(bf16[32,2,192]{2,1,0:T(2,128)(2,1)} %reshape.1034), calls=%async_computation.1 | async-start | bytes 65536 | tf_op jit(solution)/shard_map/all_to_all | solution.py:111
  39.4 0.7 %copy-start.3 = (f32[3]{0:T(128)S(1)}, f32[3]{0:T(128)}, u32[]{:S(2)}) copy-start(f32[3]{0:T(128)} %param.9) | copy-start | bytes 40
